TPU v7x, 32 devices: a whole 2x2x4 slice. The times are simulated.
32 devices in a mesh: rep: 4 (over x, core), shard: 8 (over z, y).
Axes of the slice: x: 2, y: 2, z: 4, core: 2. Of those that a mesh axis runs over, the one named last changes fastest.
Arguments:
- tokens: bfloat16 [16384, 768], P(('rep', 'shard')), may hold values from -6 to 6
- segment_ids: int32 [16384], P(('rep', 'shard')), may hold values from 0 to 511, never falling along the last dimension, each value on 1 to 512 neighbouring positions
- buckets: int32 [1023], replicated, may hold values from 0 to 31
- w_query: bfloat16 [768, 768], P('shard'), may hold values from -0.21875 to 0.21875
- w_key: bfloat16 [768, 768], P('shard'), may hold values from -0.21875 to 0.21875
- w_value: bfloat16 [768, 768], P('shard'), may hold values from -0.21875 to 0.21875
- w_output: bfloat16 [768, 768], P('shard'), may hold values from -0.625 to 0.625
- w_gate: bfloat16 [768, 2048], P('shard'), may hold values from -0.21875 to 0.21875
- w_up: bfloat16 [768, 2048], P('shard'), may hold values from -0.21875 to 0.21875
- w_down: bfloat16 [2048, 768], P('shard'), may hold values from -0.125 to 0.125
- norm_attn: bfloat16 [768], P('shard'), may hold values from 0.099609375 to 1.8984375
- norm_ffn: bfloat16 [768], P('shard'), may hold values from 0.099609375 to 1.8984375
- rel_bias: bfloat16 [32, 12], P('shard'), may hold values from -4 to 4
- cotangent: bfloat16 [16384, 768], P(('rep', 'shard')), may hold values from -6 to 6
Outputs:
- output: bfloat16 [16384, 768], P(('rep', 'shard'))
- grad_tokens: bfloat16 [16384, 768], P(('rep', 'shard'))
- grad_w_query: float32 [768, 768], P('shard')
- grad_w_key: float32 [768, 768], P('shard')
- grad_w_value: float32 [768, 768], P('shard')
- grad_w_output: float32 [768, 768], P('shard')
- grad_w_gate: float32 [768, 2048], P('shard')
- grad_w_up: float32 [768, 2048], P('shard')
- grad_w_down: float32 [2048, 768], P('shard')
- grad_norm_attn: float32 [768], P('shard')
- grad_norm_ffn: float32 [768], P('shard')
- grad_rel_bias: float32 [32, 12], P('shard')
Inputs may be any that keep to these rules, and one draw needn't show every extreme that they name: `segment_ids`: ids never fall along the bytes; a document holds 1 to 512 bytes. `buckets`: entry j - i + 511 is the bucket of key j seen from query i of one sequence.
All inputs are finite; a program needn't handle non-finite values.
Results may differ from a plain program's by a relative error of at most 0.019.
Values may be sent and summed in bfloat16 or wider, within the bound.
No kernel may reach another device: no remote copies, remote signals or barrier semaphores. Data moves between devices by JAX's collectives and lax.ppermute only.
A program may use at most 192 MiB of HBM per device.

v0:
```python
import jax
import jax.numpy as jnp
from jax import lax
from jax.sharding import PartitionSpec as P

D = 768
HEADS = 12
HD = 64
NB = 32
EPSILON = 1e-06
HIGHEST = lax.Precision.HIGHEST


def product(left_op, right_op):
    return jnp.dot(left_op, right_op, preferred_element_type=jnp.float32)


def product_tn(left_op, right_op):
    return lax.dot_general(
        left_op, right_op, (((0,), (0,)), ((), ())), preferred_element_type=jnp.float32
    )


def product_nt(left_op, right_op):
    return lax.dot_general(
        left_op, right_op, (((1,), (1,)), ((), ())), preferred_element_type=jnp.float32
    )


def gelu_tanh(values):
    return jax.nn.gelu(values, approximate=True)


def normalize(values, gain_vec):
    inverse = lax.rsqrt(jnp.mean(values * values, axis=-1, keepdims=True) + EPSILON)
    return (values * inverse * gain_vec, inverse)


def normalize_back(grad_out, values, inverse, gain_vec):
    unit_rows = values * inverse
    grad_gain = jnp.sum(grad_out * unit_rows, axis=0)
    scaled = grad_out * gain_vec
    grad_in = inverse * (scaled - unit_rows * jnp.mean(scaled * unit_rows, axis=-1, keepdims=True))
    return (grad_in, grad_gain)


def toeplitz_rows(table_low, block_start, block_rows, length):
    heads = table_low.shape[0]
    padded = jnp.pad(table_low, ((0, 0), (0, 1)))
    tiled = jnp.broadcast_to(padded[:, None, :], (heads, block_rows, 2 * length))
    flat = tiled.reshape(heads, block_rows * 2 * length)[:, : block_rows * (2 * length - 1)]
    skewed = flat.reshape(heads, block_rows, 2 * length - 1)
    return lax.dynamic_slice_in_dim(skewed, length - 1 - block_start, length, 2)


def diagonal_sums(grad_low, block_start, length):
    heads, block_rows, unused_keys = grad_low.shape
    width = 2 * length - 1 + block_rows
    zero_index = jnp.zeros((), jnp.int32)
    placed = lax.dynamic_update_slice(
        jnp.zeros((heads, block_rows, width), jnp.bfloat16),
        grad_low,
        (zero_index, zero_index, length - 1 - block_start),
    )
    flat = jnp.pad(placed.reshape(heads, block_rows * width), ((0, 0), (0, block_rows)))
    sheared = flat.reshape(heads, block_rows, width + 1)[:, :, : 2 * length - 1]
    return jnp.sum(sheared, axis=1, dtype=jnp.float32)


def block_scores(query_block, segment_block, block_start, key_rows, segment_ids, table_low):
    block_rows = query_block.shape[0]
    length = key_rows.shape[0]
    raw_scores = jnp.einsum(
        "qhd,khd->hqk", query_block, key_rows, preferred_element_type=jnp.float32
    ) * HD ** (-0.5)
    rel_terms = toeplitz_rows(table_low, block_start, block_rows, length)
    same_doc = segment_block[:, None] == segment_ids[None, :]
    return jnp.where(same_doc[None], raw_scores + rel_terms.astype(jnp.float32), -1000000000.0)


def block_inputs(queries, segment_ids):
    length = queries.shape[0]
    block_rows = min(512, length)
    block_count = length // block_rows
    return (
        queries.reshape(block_count, block_rows, HEADS, HD),
        segment_ids.reshape(block_count, block_rows),
        jnp.arange(block_count, dtype=jnp.int32) * block_rows,
    )


def forward(weights, tokens_f, segment_ids, buckets):
    (
        query_full,
        key_full,
        value_full,
        output_full,
        gate_full,
        up_full,
        down_full,
        attn_gain,
        ffn_gain,
        bias_full,
    ) = weights
    length = tokens_f.shape[0]
    normed_one, inverse_one = normalize(tokens_f, attn_gain.astype(jnp.float32))
    normed_one = normed_one.astype(jnp.bfloat16)
    queries = product(normed_one, query_full).astype(jnp.bfloat16).reshape(length, HEADS, HD)
    key_rows = product(normed_one, key_full).astype(jnp.bfloat16).reshape(length, HEADS, HD)
    value_rows = product(normed_one, value_full).astype(jnp.bfloat16).reshape(length, HEADS, HD)
    bucket_onehot = (buckets[:, None] == jnp.arange(NB, dtype=jnp.int32)[None, :]).astype(
        jnp.bfloat16
    )
    table_low = product(bucket_onehot, bias_full).T.astype(jnp.bfloat16)

    def attend(inputs):
        query_block, segment_block, block_start = inputs
        scores = block_scores(
            query_block, segment_block, block_start, key_rows, segment_ids, table_low
        )
        row_peak = jnp.max(scores, axis=-1, keepdims=True)
        weights_exp = jnp.exp(scores - row_peak)
        row_total = jnp.sum(weights_exp, axis=-1, keepdims=True)
        prob_rows = (weights_exp / row_total).astype(jnp.bfloat16)
        block_out = jnp.einsum(
            "hqk,khd->qhd", prob_rows, value_rows, preferred_element_type=jnp.float32
        )
        return (block_out.astype(jnp.bfloat16), row_peak + jnp.log(row_total))

    attended, log_total = lax.map(attend, block_inputs(queries, segment_ids))
    attended = attended.reshape(length, D)
    middle = tokens_f + product(attended, output_full)
    normed_two, inverse_two = normalize(middle, ffn_gain.astype(jnp.float32))
    normed_two = normed_two.astype(jnp.bfloat16)
    gate_pre = product(normed_two, gate_full)
    up_part = product(normed_two, up_full)
    hidden = (gelu_tanh(gate_pre) * up_part).astype(jnp.bfloat16)
    output = middle + product(hidden, down_full)
    kept_acts = (
        normed_one,
        inverse_one,
        queries,
        key_rows,
        value_rows,
        table_low,
        attended,
        log_total,
        middle,
        normed_two,
        inverse_two,
        gate_pre,
        up_part,
        hidden,
    )
    return (output, kept_acts)


def shards(
    tokens,
    segment_ids,
    buckets,
    w_query,
    w_key,
    w_value,
    w_output,
    w_gate,
    w_up,
    w_down,
    norm_attn,
    norm_ffn,
    rel_bias,
    cotangent,
):
    gathered = (
        lax.all_gather(w_query, "shard", axis=0, tiled=True),
        lax.all_gather(w_key, "shard", axis=0, tiled=True),
        lax.all_gather(w_value, "shard", axis=0, tiled=True),
        lax.all_gather(w_output, "shard", axis=0, tiled=True),
        lax.all_gather(w_gate, "shard", axis=0, tiled=True),
        lax.all_gather(w_up, "shard", axis=0, tiled=True),
        lax.all_gather(w_down, "shard", axis=0, tiled=True),
        lax.all_gather(norm_attn, "shard", axis=0, tiled=True),
        lax.all_gather(norm_ffn, "shard", axis=0, tiled=True),
        lax.all_gather(rel_bias, "shard", axis=0, tiled=True),
    )
    tokens_f = tokens.astype(jnp.float32)
    length = tokens_f.shape[0]
    output, kept_acts = forward(gathered, tokens_f, segment_ids, buckets)
    back_weights = (
        lax.all_gather(w_query, "shard", axis=0, tiled=True),
        lax.all_gather(w_key, "shard", axis=0, tiled=True),
        lax.all_gather(w_value, "shard", axis=0, tiled=True),
        lax.all_gather(w_output, "shard", axis=0, tiled=True),
        lax.all_gather(w_gate, "shard", axis=0, tiled=True),
        lax.all_gather(w_up, "shard", axis=0, tiled=True),
        lax.all_gather(w_down, "shard", axis=0, tiled=True),
        lax.all_gather(norm_attn, "shard", axis=0, tiled=True),
        lax.all_gather(norm_ffn, "shard", axis=0, tiled=True),
        lax.all_gather(rel_bias, "shard", axis=0, tiled=True),
    )
    unused_out, kept_acts = forward(back_weights, tokens_f, segment_ids, buckets)
    (
        query_full,
        key_full,
        value_full,
        output_full,
        gate_full,
        up_full,
        down_full,
        attn_gain,
        ffn_gain,
        bias_full,
    ) = back_weights
    (
        normed_one,
        inverse_one,
        queries,
        key_rows,
        value_rows,
        table_low,
        attended,
        log_total,
        middle,
        normed_two,
        inverse_two,
        gate_pre,
        up_part,
        hidden,
    ) = kept_acts
    grad_out = cotangent.astype(jnp.float32)
    grad_w_down = product_tn(hidden, cotangent)
    grad_hidden = product_nt(cotangent, down_full)
    activated, gelu_pull = jax.vjp(gelu_tanh, gate_pre)
    grad_gate = gelu_pull(grad_hidden * up_part)[0].astype(jnp.bfloat16)
    grad_up = (grad_hidden * activated).astype(jnp.bfloat16)
    grad_w_gate = product_tn(normed_two, grad_gate)
    grad_w_up = product_tn(normed_two, grad_up)
    grad_normed_two = product_nt(grad_gate, gate_full) + product_nt(grad_up, up_full)
    grad_middle_part, grad_norm_ffn = normalize_back(
        grad_normed_two, middle, inverse_two, ffn_gain.astype(jnp.float32)
    )
    grad_middle = grad_out + grad_middle_part
    grad_branch = grad_middle.astype(jnp.bfloat16)
    grad_w_output = product_tn(attended, grad_branch)
    grad_attended = (
        product_nt(grad_branch, output_full).astype(jnp.bfloat16).reshape(length, HEADS, HD)
    )
    query_blocks, segment_blocks, block_starts = block_inputs(queries, segment_ids)
    grad_att_blocks = grad_attended.reshape(query_blocks.shape)

    def attend_back(carry_acc, inputs):
        grad_keys, grad_values, grad_offsets = carry_acc
        query_block, segment_block, block_start, grad_block, log_block = inputs
        scores = block_scores(
            query_block, segment_block, block_start, key_rows, segment_ids, table_low
        )
        prob_rows = jnp.exp(scores - log_block)
        grad_probs = jnp.einsum(
            "qhd,khd->hqk", grad_block, value_rows, preferred_element_type=jnp.float32
        )
        grad_scores = prob_rows * (
            grad_probs - jnp.sum(prob_rows * grad_probs, axis=-1, keepdims=True)
        )
        grad_low = grad_scores.astype(jnp.bfloat16)
        grad_query = jnp.einsum(
            "hqk,khd->qhd", grad_low, key_rows, preferred_element_type=jnp.float32
        ) * HD ** (-0.5)
        grad_keys = grad_keys + jnp.einsum(
            "hqk,qhd->khd", grad_low, query_block, preferred_element_type=jnp.float32
        ) * HD ** (-0.5)
        grad_values = grad_values + jnp.einsum(
            "hqk,qhd->khd",
            prob_rows.astype(jnp.bfloat16),
            grad_block,
            preferred_element_type=jnp.float32,
        )
        diagonal = diagonal_sums(grad_low, block_start, length)
        return ((grad_keys, grad_values, grad_offsets + diagonal), grad_query)

    zero_rows = jnp.zeros((length, HEADS, HD), jnp.float32)
    zero_offsets = jnp.zeros((HEADS, 2 * length - 1), jnp.float32)
    (grad_keys, grad_values, grad_offsets), grad_q_blocks = lax.scan(
        attend_back,
        (zero_rows, zero_rows, zero_offsets),
        (query_blocks, segment_blocks, block_starts, grad_att_blocks, log_total),
    )
    grad_queries = grad_q_blocks.reshape(length, D).astype(jnp.bfloat16)
    grad_key_rows = grad_keys.reshape(length, D).astype(jnp.bfloat16)
    grad_value_rows = grad_values.reshape(length, D).astype(jnp.bfloat16)
    grad_w_query = product_tn(normed_one, grad_queries)
    grad_w_key = product_tn(normed_one, grad_key_rows)
    grad_w_value = product_tn(normed_one, grad_value_rows)
    grad_normed_one = (
        product_nt(grad_queries, query_full)
        + product_nt(grad_key_rows, key_full)
        + product_nt(grad_value_rows, value_full)
    )
    grad_tokens_part, grad_norm_attn = normalize_back(
        grad_normed_one, tokens_f, inverse_one, attn_gain.astype(jnp.float32)
    )
    grad_tokens = (grad_middle + grad_tokens_part).astype(jnp.bfloat16)
    bucket_onehot = (buckets[:, None] == jnp.arange(NB, dtype=jnp.int32)[None, :]).astype(
        jnp.float32
    )
    grad_rel_bias = jnp.dot(
        bucket_onehot.T, grad_offsets.T, precision=HIGHEST, preferred_element_type=jnp.float32
    )
    (
        share_query,
        share_key,
        share_value,
        share_output,
        share_gate,
        share_up,
        share_down,
        share_attn,
        share_ffn,
        share_bias,
    ) = (
        lax.psum_scatter(
            grad_w_query.astype(jnp.bfloat16), "shard", scatter_dimension=0, tiled=True
        ).astype(jnp.float32),
        lax.psum_scatter(
            grad_w_key.astype(jnp.bfloat16), "shard", scatter_dimension=0, tiled=True
        ).astype(jnp.float32),
        lax.psum_scatter(
            grad_w_value.astype(jnp.bfloat16), "shard", scatter_dimension=0, tiled=True
        ).astype(jnp.float32),
        lax.psum_scatter(
            grad_w_output.astype(jnp.bfloat16), "shard", scatter_dimension=0, tiled=True
        ).astype(jnp.float32),
        lax.psum_scatter(
            grad_w_gate.astype(jnp.bfloat16), "shard", scatter_dimension=0, tiled=True
        ).astype(jnp.float32),
        lax.psum_scatter(
            grad_w_up.astype(jnp.bfloat16), "shard", scatter_dimension=0, tiled=True
        ).astype(jnp.float32),
        lax.psum_scatter(
            grad_w_down.astype(jnp.bfloat16), "shard", scatter_dimension=0, tiled=True
        ).astype(jnp.float32),
        lax.psum_scatter(
            grad_norm_attn.astype(jnp.bfloat16), "shard", scatter_dimension=0, tiled=True
        ).astype(jnp.float32),
        lax.psum_scatter(
            grad_norm_ffn.astype(jnp.bfloat16), "shard", scatter_dimension=0, tiled=True
        ).astype(jnp.float32),
        lax.psum_scatter(
            grad_rel_bias.astype(jnp.bfloat16), "shard", scatter_dimension=0, tiled=True
        ).astype(jnp.float32),
    )
    totals = (
        lax.psum(share_query.astype(jnp.bfloat16), "rep").astype(jnp.float32),
        lax.psum(share_key.astype(jnp.bfloat16), "rep").astype(jnp.float32),
        lax.psum(share_value.astype(jnp.bfloat16), "rep").astype(jnp.float32),
        lax.psum(share_output.astype(jnp.bfloat16), "rep").astype(jnp.float32),
        lax.psum(share_gate.astype(jnp.bfloat16), "rep").astype(jnp.float32),
        lax.psum(share_up.astype(jnp.bfloat16), "rep").astype(jnp.float32),
        lax.psum(share_down.astype(jnp.bfloat16), "rep").astype(jnp.float32),
        lax.psum(share_attn.astype(jnp.bfloat16), "rep").astype(jnp.float32),
        lax.psum(share_ffn.astype(jnp.bfloat16), "rep").astype(jnp.float32),
        lax.psum(share_bias.astype(jnp.bfloat16), "rep").astype(jnp.float32),
    )
    return (
        output.astype(jnp.bfloat16),
        grad_tokens,
        totals[0],
        totals[1],
        totals[2],
        totals[3],
        totals[4],
        totals[5],
        totals[6],
        totals[7],
        totals[8],
        totals[9],
    )


def solution(mesh):
    return jax.shard_map(
        shards,
        mesh=mesh,
        in_specs=(
            P(("rep", "shard"), None),
            P(("rep", "shard")),
            P(),
            P("shard", None),
            P("shard", None),
            P("shard", None),
            P("shard", None),
            P("shard", None),
            P("shard", None),
            P("shard", None),
            P("shard"),
            P("shard"),
            P("shard", None),
            P(("rep", "shard"), None),
        ),
        out_specs=(
            P(("rep", "shard"), None),
            P(("rep", "shard"), None),
            P("shard", None),
            P("shard", None),
            P("shard", None),
            P("shard", None),
            P("shard", None),
            P("shard", None),
            P("shard", None),
            P("shard"),
            P("shard"),
            P("shard", None),
        ),
        check_vma=False,
    )
```

profile of v0, /device:TPU:0, one launch (start us, length us, event | category | flops | bytes accessed | tf_op | source)
XLA Modules:
  0.0 968.3 jit_solution(6518679605670658426)
XLA Ops:
  15.6 23.2 %all-reduce.9 = (bf16[768]{0:T(1024)(128)(2,1)S(1)}, bf16[768]{0:T(1024)(128)(2,1)S(1)}) all-reduce(bf16[768]{0:T(1024)(128)(2,1)S(1)} %dynamic-update-slice, bf16[768]{0:T(1024)(128)(2,1)S(1)} %dynamic-update-slice.1), channel_id=1, replica_groups=mesh['rep'=4,'shard'=8] {'shard'}, use_global_device_ids=true, to_apply=%add.3 | all-reduce | flops 1536 | bytes 6144
  39.1 16.5 %all-gather = bf16[8,4,12]{2,1,0:T(4,128)(2,1)S(1)} all-gather(bf16[1,4,12]{2,1,0:T(4,128)(2,1)S(1)} %bitcast.97), channel_id=1, replica_groups=mesh['rep'=4,'shard'=8] {'shard'}, dimensions={0}, use_global_device_ids=true | all-gather | bytes 864 | tf_op jit(solution)/shard_map/all_gather | solution.py:184
  67.8 29.2 %copy.64 = bf16[2,8,512,1024]{3,1,2,0:T(8,128)(2,1)S(1)} copy(bf16[2,8,512,1024]{3,2,1,0:T(8,128)(2,1)S(1)} %bitcast.78) | data formatting | bytes 33554432
  103.7 36.8 %reshape.147 = bf16[12,512,1023]{2,1,0:T(8,128)(2,1)} reshape(bf16[12,523776]{1,0:T(8,128)(2,1)} %slice.15) | data formatting | bytes 25141248 | tf_op jit(solution)/shard_map/while/body/eval_jaxpr/reshape | solution.py:52
  140.4 9.7 %dynamic_slice.35 = bf16[12,512,512]{2,1,0:T(8,128)(2,1)} slice(bf16[12,512,1023]{2,1,0:T(8,128)(2,1)} %reshape.147), slice={[0:12], [0:512], [511:1023]} | slice | bytes 12582912 | tf_op jit(solution)/shard_map/while/body/eval_jaxpr/dynamic_slice | solution.py:53
  150.2 8.7 copy.62
  185.3 55.6 %all-gather.17.cloned.1.call-done = bf16[768,2048]{1,0:T(8,128)(2,1)} async-done(((bf16[96,2048]{1,0:T(8,128)(2,1)}), bf16[768,2048]{1,0:T(8,128)(2,1)}) %all-gather.17.cloned.1.call-update) | async-done | bytes 3145744 | tf_op jit(solution)/shard_map/all_gather | solution.py:179
  246.6 55.1 %all-gather.19.cloned.1.call-done = bf16[768,2048]{1,0:T(8,128)(2,1)} async-done(((bf16[96,2048]{1,0:T(8,128)(2,1)}), bf16[768,2048]{1,0:T(8,128)(2,1)}) %all-gather.19.cloned.1.call-update) | async-done | bytes 3145744 | tf_op jit(solution)/shard_map/all_gather | solution.py:180
  307.4 55.2 %all-gather.21.cloned.1.call-done = bf16[2048,768]{1,0:T(8,128)(2,1)} async-done(((bf16[256,768]{1,0:T(8,128)(2,1)}), bf16[2048,768]{1,0:T(8,128)(2,1)}) %all-gather.21.cloned.1.call-update) | async-done | bytes 3145744 | tf_op jit(solution)/shard_map/all_gather | solution.py:181
  362.6 8.7 multiply_convert_fusion.1
  381.7 10.6 %multiply_reduce_fusion = (f32[12,512]{1,0:T(8,128)S(1)}, f32[12,512,512]{1,2,0:T(8,128)}) fusion(f32[12,512,512]{1,2,0:T(8,128)} %copy-done, f32[12,512]{1,0:T(8,128)S(1)} %log_add_fusion, bf16[512,12,64]{0,2,1:T(8,128)(2,1)S(1)} %bitcast.82, bf16[512,12,64]{0,2,1:T(8,128)(2,1)} %bitcast.87), kind=kOutput, calls=%fused_computation.2 | convolution fusion | flops 412084224 | bytes 26787840 | tf_op jit(solution)/shard_map/while/body/eval_jaxpr/qhd,khd->hqk/dot_general | solution.py:258
  445.9 8.7 copy.63
  454.5 9.3 dynamic_update_slice.15.clone
  463.9 69.5 %reshape.149 = bf16[12,785920]{1,0:T(8,128)(2,1)} reshape(bf16[12,512,1535]{2,1,0:T(8,128)(2,1)} %dynamic_update_slice.15.clone) | data formatting | bytes 37724160 | tf_op jit(solution)/shard_map/while/body/eval_jaxpr/reshape | solution.py:65
  533.4 13.1 %pad.16 = bf16[12,786432]{1,0:T(8,128)(2,1)S(1)} pad(bf16[12,785920]{1,0:T(8,128)(2,1)} %reshape.149, bf16[]{:T(256)} %constant.111.clone.1), padding=0_0x0_512 | pad | bytes 37736448 | tf_op jit(solution)/shard_map/while/body/eval_jaxpr/jit(_pad)/pad | solution.py:65
  546.5 19.4 %copy.65 = bf16[2,8,512,1536]{3,2,1,0:T(8,128)(2,1)} copy(bf16[2,8,512,1536]{3,1,2,0:T(8,128)(2,1)S(1)} %bitcast.76) | data formatting | bytes 50331648
  565.9 16.7 %slice.17 = bf16[12,512,1536]{2,1,0:T(8,128)(2,1)} slice(bf16[16,512,1536]{2,1,0:T(8,128)(2,1)} %bitcast.77), slice={[0:12], [0:512], [0:1536]} | slice | bytes 37748736 | tf_op jit(solution)/shard_map/while/body/eval_jaxpr/reshape | solution.py:66
  582.5 7.8 convert_reduce_fusion
  597.0 34.9 %all-reduce.8 = (bf16[768]{0:T(1024)(128)(2,1)S(1)}, bf16[768]{0:T(1024)(128)(2,1)S(1)}, bf16[32,12]{1,0:T(8,128)(2,1)S(1)}) all-reduce(bf16[768]{0:T(1024)(128)(2,1)S(1)} %get-tuple-element.78, bf16[768]{0:T(1024)(128)(2,1)S(1)} %get-tuple-element.76, ...), channel_id=9, replica_groups=mesh['rep'=4,'shard'=8] {'shard'}, use_global_device_ids=true, to_apply=%region_22.23.clone | all-reduce | flops 1920 | bytes 7680
  639.8 32.4 %reduce-scatter.14.cloned.1.call-done = bf16[96,768]{1,0:T(8,128)(2,1)} async-done(((bf16[768,768]{1,0:T(8,128)(2,1)}), bf16[96,768]{1,0:T(8,128)(2,1)}) %reduce-scatter.14.cloned.1.call-update) | async-done | bytes 147472 | tf_op jit(solution)/shard_map/reduce_scatter | solution.py:329
  672.2 77.1 %reduce-scatter.16.cloned.1.call-done = bf16[96,2048]{1,0:T(8,128)(2,1)} async-done(((bf16[768,2048]{1,0:T(8,128)(2,1)}), bf16[96,2048]{1,0:T(8,128)(2,1)}) %reduce-scatter.16.cloned.1.call-update) | async-done | bytes 393232 | tf_op jit(solution)/shard_map/reduce_scatter | solution.py:332
  749.3 76.8 %reduce-scatter.18.cloned.1.call-done = bf16[96,2048]{1,0:T(8,128)(2,1)} async-done(((bf16[768,2048]{1,0:T(8,128)(2,1)}), bf16[96,2048]{1,0:T(8,128)(2,1)}) %reduce-scatter.18.cloned.1.call-update) | async-done | bytes 393232 | tf_op jit(solution)/shard_map/reduce_scatter | solution.py:335
  826.1 76.8 %reduce-scatter.20.cloned.1.call-done = bf16[256,768]{1,0:T(8,128)(2,1)} async-done(((bf16[2048,768]{1,0:T(8,128)(2,1)}), bf16[256,768]{1,0:T(8,128)(2,1)}) %reduce-scatter.20.cloned.1.call-update) | async-done | bytes 393232 | tf_op jit(solution)/shard_map/reduce_scatter | solution.py:338
  910.2 40.8 %all-reduce.14.cloned.1.call-done = (bf16[96,768]{1,0:T(8,128)(2,1)}, bf16[96,768]{1,0:T(8,128)(2,1)}, bf16[96,768]{1,0:T(8,128)(2,1)}, bf16[96,768]{1,0:T(8,128...) async-done(((bf16[96,768]{1,0:T(8,128)(2,1)}, bf16[96,768]{1,0:T(8,128)(2,1)}, bf16[96,768]{1,0:T(8,128)(2,1)}, ...) | async-done | bytes 1769488 | tf_op jit(solution)/shard_map/psum | solution.py:352
  (184 shorter events, 158.9 us)
Async XLA Ops:
  7.2 31.6 %copy-start.2 = (bf16[512,768]{1,0:T(8,128)(2,1)S(1)}, bf16[512,768]{1,0:T(8,128)(2,1)}, u32[]{:S(2)}) copy-start(bf16[512,768]{1,0:T(8,128)(2,1)} %param.14) | copy-start | bytes 2359300
  7.2 31.9 %copy-start.26 = (bf16[4,12]{1,0:T(4,128)(2,1)S(1)}, bf16[4,12]{1,0:T(4,128)(2,1)}, u32[]{:S(2)}) copy-start(bf16[4,12]{1,0:T(4,128)(2,1)} %param.26) | copy-start | bytes 292
  7.2 48.3 %copy-start.32 = (s32[1023]{0:T(1024)S(1)}, s32[1023]{0:T(1024)}, u32[]{:S(2)}) copy-start(s32[1023]{0:T(1024)} %param.16) | copy-start | bytes 12280
  7.2 151.9 %all-gather.9.cloned.1.call-start = ((), (), s32[]{:S(2)}) async-start(), calls=%async_computation.7 | async-start | bytes 1327104 | tf_op jit(solution)/shard_map/all_gather | solution.py:177
  7.9 153.3 %all-gather.11.cloned.1.call-start = ((), (), s32[]{:S(2)}) async-start(), calls=%async_computation.8 | async-start | bytes 1327104 | tf_op jit(solution)/shard_map/all_gather | solution.py:175
  8.7 155.3 %all-gather.13.cloned.1.call-start = ((), (), s32[]{:S(2)}) async-start(), calls=%async_computation.9 | async-start | bytes 1327104 | tf_op jit(solution)/shard_map/all_gather | solution.py:176
  9.4 172.0 %all-gather.15.cloned.1.call-start = ((), (), s32[]{:S(2)}) async-start(), calls=%async_computation.10 | async-start | bytes 1327104 | tf_op jit(solution)/shard_map/all_gather | solution.py:178
  10.0 231.0 %all-gather.17.cloned.1.call-start = ((), (), s32[]{:S(2)}) async-start(), calls=%async_computation.11 | async-start | bytes 3538944 | tf_op jit(solution)/shard_map/all_gather | solution.py:179
  10.6 291.1 %all-gather.19.cloned.1.call-start = ((), (), s32[]{:S(2)}) async-start(), calls=%async_computation.12 | async-start | bytes 3538944 | tf_op jit(solution)/shard_map/all_gather | solution.py:180
  11.2 351.4 %all-gather.21.cloned.1.call-start = ((), (), s32[]{:S(2)}) async-start(), calls=%async_computation.13 | async-start | bytes 3538944 | tf_op jit(solution)/shard_map/all_gather | solution.py:181
  11.9 627.9 %reduce-scatter.8.cloned.1.call-start = ((), (), s32[]{:S(2)}) async-start(), calls=%async_computation.14 | async-start | bytes 1327104 | tf_op jit(solution)/shard_map/reduce_scatter | solution.py:320
  163.7 12.2 %copy-start.9 = (bf16[512,768]{0,1:T(8,128)(2,1)}, bf16[512,768]{0,1:T(8,128)(2,1)S(1)}, u32[]{:S(2)}) copy-start(bf16[512,768]{0,1:T(8,128)(2,1)S(1)} %copy.48) | copy-start | bytes 2359300
  185.3 116.4 %copy-start.17 = (bf16[512,768]{1,0:T(8,128)(2,1)}, bf16[512,768]{1,0:T(8,128)(2,1)S(1)}, u32[]{:S(2)}) copy-start(bf16[512,768]{1,0:T(8,128)(2,1)S(1)} %multiply_convert_fusion.5) | copy-start | bytes 2359300
  246.6 116.0 %copy-start.19 = (bf16[512,768]{1,0:T(8,128)(2,1)S(1)}, bf16[512,768]{1,0:T(8,128)(2,1)}, u32[]{:S(2)}) copy-start(bf16[512,768]{1,0:T(8,128)(2,1)} %param.27) | copy-start | bytes 2359300
  381.7 10.7 %slice-start = ((s8[12582912]{0:T(1024)(128)(4,1)}), s8[4194304]{0:T(1024)(128)(4,1)S(1)}, s32[]{:S(2)}) async-start(s8[12582912]{0:T(1024)(128)(4,1)} %bitcast.74), calls=%async_computation.22 | async-start | bytes 8388608
  381.7 11.6 %slice-start.1 = ((s8[12582912]{0:T(1024)(128)(4,1)}), s8[4194304]{0:T(1024)(128)(4,1)S(1)}, s32[]{:S(2)}) async-start(s8[12582912]{0:T(1024)(128)(4,1)} %bitcast.74), calls=%async_computation.23 | async-start | bytes 8388608
  381.7 12.8 %slice-start.2 = ((s8[12582912]{0:T(1024)(128)(4,1)}), s8[4194304]{0:T(1024)(128)(4,1)S(1)}, s32[]{:S(2)}) async-start(s8[12582912]{0:T(1024)(128)(4,1)} %bitcast.74), calls=%async_computation.24 | async-start | bytes 8388608
  407.0 232.8 %reduce-scatter.10.cloned.1.call-start = ((), (), s32[]{:S(2)}) async-start(), calls=%async_computation.15 | async-start | bytes 1327104 | tf_op jit(solution)/shard_map/reduce_scatter | solution.py:323
  415.1 224.7 %reduce-scatter.12.cloned.1.call-start = ((), (), s32[]{:S(2)}) async-start(), calls=%async_computation.16 | async-start | bytes 1327104 | tf_op jit(solution)/shard_map/reduce_scatter | solution.py:326
  424.7 247.5 %reduce-scatter.14.cloned.1.call-start = ((), (), s32[]{:S(2)}) async-start(), calls=%async_computation.17 | async-start | bytes 1327104 | tf_op jit(solution)/shard_map/reduce_scatter | solution.py:329
  426.6 322.7 %reduce-scatter.16.cloned.1.call-start = ((), (), s32[]{:S(2)}) async-start(), calls=%async_computation.18 | async-start | bytes 3538944 | tf_op jit(solution)/shard_map/reduce_scatter | solution.py:332
  432.1 394.0 %reduce-scatter.18.cloned.1.call-start = ((), (), s32[]{:S(2)}) async-start(), calls=%async_computation.19 | async-start | bytes 3538944 | tf_op jit(solution)/shard_map/reduce_scatter | solution.py:335
  438.3 464.6 %reduce-scatter.20.cloned.1.call-start = ((), (), s32[]{:S(2)}) async-start(), calls=%async_computation.20 | async-start | bytes 3538944 | tf_op jit(solution)/shard_map/reduce_scatter | solution.py:338
  444.5 506.5 %all-reduce.14.cloned.1.call-start = ((), (), s32[]{:S(2)}) async-start(), calls=%async_computation.21 | async-start | bytes 3538944 | tf_op jit(solution)/shard_map/psum | solution.py:352
  (30 other events, 109.6 us)
Sparse Core Ops, SparseCore 0:
  10.2 43.9 all-gather.8
  56.4 39.8 all-gather.10
  98.5 39.7 all-gather.12
  140.3 39.7 all-gather.14
  182.2 58.7 all-gather.16
  243.0 58.6 all-gather.18
  303.9 58.6 all-gather.20
  407.2 63.4 reduce-scatter.7
  474.0 63.7 reduce-scatter.9
  541.1 63.8 reduce-scatter.11
  608.4 63.8 reduce-scatter.13
  675.7 73.5 reduce-scatter.15
  752.9 73.1 reduce-scatter.17
  829.6 73.3 reduce-scatter.19
  905.7 45.3 all-reduce.13
where the time goes:
time: 973 us; the launch traced here: 968 us
  waiting for transfers between devices  475 us (49%)
  local copies, waits for them, and re-layouts  262 us (27%)
  matrix products  101 us (10%)
  blocking collectives  80.6 us (8%)
  other arithmetic  32.6 us (3%)
  between operations  16.7 us (2%)
    unnamed x91, local copies, waits for them, and re-layouts  90.8 us
    reduce_scatter x1, waiting for transfers between devices, shards(): lax.psum_scatter(grad_w_gate.astype(jnp.bfloat16), 'shard', scatter_dimen...  77.1 us
    reduce_scatter x1, waiting for transfers between devices, shards(): lax.psum_scatter(grad_w_down.astype(jnp.bfloat16), 'shard', scatter_dimen...  76.8 us
    reduce_scatter x1, waiting for transfers between devices, shards(): lax.psum_scatter(grad_w_up.astype(jnp.bfloat16), 'shard', scatter_dimensi...  76.8 us
    reshape x1, local copies, waits for them, and re-layouts, diagonal_sums(): placed.reshape(heads, block_rows * width)  69.5 us
    unnamed x2, blocking collectives  58.1 us
    all_gather x1, waiting for transfers between devices, shards(): lax.all_gather(w_gate, 'shard', axis=0, tiled=True)  55.6 us
    all_gather x1, waiting for transfers between devices, shards(): lax.all_gather(w_down, 'shard', axis=0, tiled=True)  55.2 us
  transfers between devices with their start and end apart: 15, of which 8 were waited for; matrix products, arithmetic and copies ran while one was open for 34% of the time, Pallas kernels for 0%

commit v1 on v0

--- a/solution.py
+++ b/solution.py
@@ -171,6 +171,12 @@
     rel_bias,
     cotangent,
 ):
+
+    def rest_the_loads(mat, comm_axis):
+        a_next = jnp.stack(lax.psum(1, comm_axis) * [mat], axis=0)
+        x_next = lax.all_to_all(a_next, comm_axis, 0, 0)
+        return jnp.concatenate(x_next, axis=0)
+
     gathered = (
         lax.all_gather(w_query, "shard", axis=0, tiled=True),
         lax.all_gather(w_key, "shard", axis=0, tiled=True),
@@ -178,7 +184,7 @@
         lax.all_gather(w_output, "shard", axis=0, tiled=True),
         lax.all_gather(w_gate, "shard", axis=0, tiled=True),
         lax.all_gather(w_up, "shard", axis=0, tiled=True),
-        lax.all_gather(w_down, "shard", axis=0, tiled=True),
+        rest_the_loads(w_down, "shard"),
         lax.all_gather(norm_attn, "shard", axis=0, tiled=True),
         lax.all_gather(norm_ffn, "shard", axis=0, tiled=True),
         lax.all_gather(rel_bias, "shard", axis=0, tiled=True),

time: 973 us -> 1000 us (1.028)
  waiting for transfers between devices: 475 us -> 494 us
    reduce_scatter x1, waiting for transfers between devices: 32.4 us -> 53 us  [shards(): lax.psum_scatter(grad_w_output.astype(jnp.bfloat16), 'shard', scatter_dim...]
    unnamed x91 -> x89, local copies, waits for them, and re-layouts: 90.8 us -> 91.8 us
  transfers between devices with their start and end apart: 15 -> 16, of which waited for: 8 -> 8; matrix products, arithmetic and copies ran while one was open for 34% -> 34% of each run, Pallas kernels for 0% -> 0%
where the time goes in v1:
time: 1000 us; the launch traced here: 998 us
  waiting for transfers between devices  494 us (49%)
  local copies, waits for them, and re-layouts  265 us (26%)
  matrix products  102 us (10%)
  blocking collectives  82.7 us (8%)
  other arithmetic  32.5 us (3%)
  between operations  16.7 us (2%)
    unnamed x89, local copies, waits for them, and re-layouts  91.8 us
    reduce_scatter x1, waiting for transfers between devices, shards(): lax.psum_scatter(grad_w_down.astype(jnp.bfloat16), 'shard', scatter_dimen...  77 us
    reduce_scatter x1, waiting for transfers between devices, shards(): lax.psum_scatter(grad_w_up.astype(jnp.bfloat16), 'shard', scatter_dimensi...  76.9 us
    reduce_scatter x1, waiting for transfers between devices, shards(): lax.psum_scatter(grad_w_gate.astype(jnp.bfloat16), 'shard', scatter_dimen...  76.8 us
    reshape x1, local copies, waits for them, and re-layouts, diagonal_sums(): placed.reshape(heads, block_rows * width)  69.5 us
    unnamed x2, blocking collectives  60.6 us
    all_gather x1, waiting for transfers between devices, shards(): lax.all_gather(w_gate, 'shard', axis=0, tiled=True)  55.6 us
    all_gather x1, waiting for transfers between devices, shards(): lax.all_gather(w_down, 'shard', axis=0, tiled=True)  55.2 us
  transfers between devices with their start and end apart: 16, of which 8 were waited for; matrix products, arithmetic and copies ran while one was open for 34% of the time, Pallas kernels for 0%

profile of v1, /device:TPU:0, one launch (start us, length us, event | category | flops | bytes accessed | tf_op | source)
XLA Modules:
  0.0 998.2 jit_solution(10827685663267182535)
XLA Ops:
  15.6 23.2 %all-reduce.9 = (bf16[768]{0:T(1024)(128)(2,1)S(1)}, bf16[768]{0:T(1024)(128)(2,1)S(1)}) all-reduce(bf16[768]{0:T(1024)(128)(2,1)S(1)} %dynamic-update-slice, bf16[768]{0:T(1024)(128)(2,1)S(1)} %dynamic-update-slice.1), channel_id=1, replica_groups=mesh['rep'=4,'shard'=8] {'shard'}, use_global_device_ids=true, to_apply=%add.3 | all-reduce | flops 1536 | bytes 6144
  39.1 16.5 %all-gather = bf16[8,4,12]{2,1,0:T(4,128)(2,1)S(1)} all-gather(bf16[1,4,12]{2,1,0:T(4,128)(2,1)S(1)} %bitcast.98), channel_id=1, replica_groups=mesh['rep'=4,'shard'=8] {'shard'}, dimensions={0}, use_global_device_ids=true | all-gather | bytes 864 | tf_op jit(solution)/shard_map/all_gather | solution.py:190
  67.9 29.2 %copy.64 = bf16[2,8,512,1024]{3,1,2,0:T(8,128)(2,1)S(1)} copy(bf16[2,8,512,1024]{3,2,1,0:T(8,128)(2,1)S(1)} %bitcast.79) | data formatting | bytes 33554432
  103.7 36.8 %reshape.152 = bf16[12,512,1023]{2,1,0:T(8,128)(2,1)} reshape(bf16[12,523776]{1,0:T(8,128)(2,1)} %slice.15) | data formatting | bytes 25141248 | tf_op jit(solution)/shard_map/while/body/eval_jaxpr/reshape | solution.py:52
  140.4 9.7 dynamic_slice.35
  150.2 8.7 copy.62
  185.3 55.6 %all-gather.17.cloned.1.call-done = bf16[768,2048]{1,0:T(8,128)(2,1)} async-done(((bf16[96,2048]{1,0:T(8,128)(2,1)}), bf16[768,2048]{1,0:T(8,128)(2,1)}) %all-gather.17.cloned.1.call-update) | async-done | bytes 3145744 | tf_op jit(solution)/shard_map/all_gather | solution.py:185
  246.6 55.1 %all-gather.19.cloned.1.call-done = bf16[768,2048]{1,0:T(8,128)(2,1)} async-done(((bf16[96,2048]{1,0:T(8,128)(2,1)}), bf16[768,2048]{1,0:T(8,128)(2,1)}) %all-gather.19.cloned.1.call-update) | async-done | bytes 3145744 | tf_op jit(solution)/shard_map/all_gather | solution.py:186
  307.4 55.2 %all-gather.21.cloned.1.call-done = bf16[2048,768]{1,0:T(8,128)(2,1)} async-done(((bf16[256,768]{1,0:T(8,128)(2,1)}), bf16[2048,768]{1,0:T(8,128)(2,1)}) %all-gather.21.cloned.1.call-update) | async-done | bytes 3145744 | tf_op jit(solution)/shard_map/all_gather | solution.py:202
  362.6 8.6 multiply_convert_fusion.1
  381.7 10.6 %multiply_reduce_fusion = (f32[12,512]{1,0:T(8,128)S(1)}, f32[12,512,512]{1,2,0:T(8,128)}) fusion(f32[12,512,512]{1,2,0:T(8,128)} %copy-done, f32[12,512]{1,0:T(8,128)S(1)} %log_add_fusion, bf16[512,12,64]{0,2,1:T(8,128)(2,1)S(1)} %bitcast.83, bf16[512,12,64]{0,2,1:T(8,128)(2,1)} %bitcast.88), kind=kOutput, calls=%fused_computation.2 | convolution fusion | flops 412084224 | bytes 26787840 | tf_op jit(solution)/shard_map/while/body/eval_jaxpr/qhd,khd->hqk/dot_general | solution.py:264
  453.1 8.7 copy.63
  461.8 9.4 dynamic_update_slice.15.clone
  471.2 69.5 %reshape.155 = bf16[12,785920]{1,0:T(8,128)(2,1)} reshape(bf16[12,512,1535]{2,1,0:T(8,128)(2,1)} %dynamic_update_slice.15.clone) | data formatting | bytes 37724160 | tf_op jit(solution)/shard_map/while/body/eval_jaxpr/reshape | solution.py:65
  540.6 13.1 %pad.16 = bf16[12,786432]{1,0:T(8,128)(2,1)S(1)} pad(bf16[12,785920]{1,0:T(8,128)(2,1)} %reshape.155, bf16[]{:T(256)} %constant.111.clone.1), padding=0_0x0_512 | pad | bytes 37736448 | tf_op jit(solution)/shard_map/while/body/eval_jaxpr/jit(_pad)/pad | solution.py:65
  553.7 19.4 %copy.65 = bf16[2,8,512,1536]{3,2,1,0:T(8,128)(2,1)} copy(bf16[2,8,512,1536]{3,1,2,0:T(8,128)(2,1)S(1)} %bitcast.77) | data formatting | bytes 50331648
  573.2 16.6 %slice.17 = bf16[12,512,1536]{2,1,0:T(8,128)(2,1)} slice(bf16[16,512,1536]{2,1,0:T(8,128)(2,1)} %bitcast.78), slice={[0:12], [0:512], [0:1536]} | slice | bytes 37748736 | tf_op jit(solution)/shard_map/while/body/eval_jaxpr/reshape | solution.py:66
  589.8 7.8 convert_reduce_fusion
  604.3 37.5 %all-reduce.8 = (bf16[768]{0:T(1024)(128)(2,1)S(1)}, bf16[768]{0:T(1024)(128)(2,1)S(1)}, bf16[32,12]{1,0:T(8,128)(2,1)S(1)}) all-reduce(bf16[768]{0:T(1024)(128)(2,1)S(1)} %get-tuple-element.78, bf16[768]{0:T(1024)(128)(2,1)S(1)} %get-tuple-element.76, ...), channel_id=9, replica_groups=mesh['rep'=4,'shard'=8] {'shard'}, use_global_device_ids=true, to_apply=%region_22.23.clone | all-reduce | flops 1920 | bytes 7680
  649.2 53.0 %reduce-scatter.14.cloned.1.call-done = bf16[96,768]{1,0:T(8,128)(2,1)} async-done(((bf16[768,768]{1,0:T(8,128)(2,1)}), bf16[96,768]{1,0:T(8,128)(2,1)}) %reduce-scatter.14.cloned.1.call-update) | async-done | bytes 147472 | tf_op jit(solution)/shard_map/reduce_scatter | solution.py:335
  702.2 76.8 %reduce-scatter.16.cloned.1.call-done = bf16[96,2048]{1,0:T(8,128)(2,1)} async-done(((bf16[768,2048]{1,0:T(8,128)(2,1)}), bf16[96,2048]{1,0:T(8,128)(2,1)}) %reduce-scatter.16.cloned.1.call-update) | async-done | bytes 393232 | tf_op jit(solution)/shard_map/reduce_scatter | solution.py:338
  779.0 76.9 %reduce-scatter.18.cloned.1.call-done = bf16[96,2048]{1,0:T(8,128)(2,1)} async-done(((bf16[768,2048]{1,0:T(8,128)(2,1)}), bf16[96,2048]{1,0:T(8,128)(2,1)}) %reduce-scatter.18.cloned.1.call-update) | async-done | bytes 393232 | tf_op jit(solution)/shard_map/reduce_scatter | solution.py:341
  855.9 77.0 %reduce-scatter.20.cloned.1.call-done = bf16[256,768]{1,0:T(8,128)(2,1)} async-done(((bf16[2048,768]{1,0:T(8,128)(2,1)}), bf16[256,768]{1,0:T(8,128)(2,1)}) %reduce-scatter.20.cloned.1.call-update) | async-done | bytes 393232 | tf_op jit(solution)/shard_map/reduce_scatter | solution.py:344
  941.3 39.6 %all-reduce.14.cloned.1.call-done = (bf16[96,768]{1,0:T(8,128)(2,1)}, bf16[96,768]{1,0:T(8,128)(2,1)}, bf16[96,768]{1,0:T(8,128)(2,1)}, bf16[96,768]{1,0:T(8,128...) async-done(((bf16[96,768]{1,0:T(8,128)(2,1)}, bf16[96,768]{1,0:T(8,128)(2,1)}, bf16[96,768]{1,0:T(8,128)(2,1)}, ...) | async-done | bytes 1769488 | tf_op jit(solution)/shard_map/psum | solution.py:358
  (185 shorter events, 167.0 us)
Async XLA Ops:
  7.2 31.6 %copy-start.2 = (bf16[512,768]{1,0:T(8,128)(2,1)S(1)}, bf16[512,768]{1,0:T(8,128)(2,1)}, u32[]{:S(2)}) copy-start(bf16[512,768]{1,0:T(8,128)(2,1)} %param.14) | copy-start | bytes 2359300
  7.2 31.9 %copy-start.26 = (bf16[4,12]{1,0:T(4,128)(2,1)S(1)}, bf16[4,12]{1,0:T(4,128)(2,1)}, u32[]{:S(2)}) copy-start(bf16[4,12]{1,0:T(4,128)(2,1)} %param.26) | copy-start | bytes 292
  7.2 48.3 %copy-start.31 = (s32[1023]{0:T(1024)S(1)}, s32[1023]{0:T(1024)}, u32[]{:S(2)}) copy-start(s32[1023]{0:T(1024)} %param.16) | copy-start | bytes 12280
  7.2 151.9 %all-gather.9.cloned.1.call-start = ((), (), s32[]{:S(2)}) async-start(), calls=%async_computation.8 | async-start | bytes 1327104 | tf_op jit(solution)/shard_map/all_gather | solution.py:183
  7.9 153.3 %all-gather.11.cloned.1.call-start = ((), (), s32[]{:S(2)}) async-start(), calls=%async_computation.9 | async-start | bytes 1327104 | tf_op jit(solution)/shard_map/all_gather | solution.py:181
  8.7 155.3 %all-gather.13.cloned.1.call-start = ((), (), s32[]{:S(2)}) async-start(), calls=%async_computation.10 | async-start | bytes 1327104 | tf_op jit(solution)/shard_map/all_gather | solution.py:182
  9.4 172.0 %all-gather.15.cloned.1.call-start = ((), (), s32[]{:S(2)}) async-start(), calls=%async_computation.11 | async-start | bytes 1327104 | tf_op jit(solution)/shard_map/all_gather | solution.py:184
  10.0 231.0 %all-gather.17.cloned.1.call-start = ((), (), s32[]{:S(2)}) async-start(), calls=%async_computation.12 | async-start | bytes 3538944 | tf_op jit(solution)/shard_map/all_gather | solution.py:185
  10.6 291.1 %all-gather.19.cloned.1.call-start = ((), (), s32[]{:S(2)}) async-start(), calls=%async_computation.13 | async-start | bytes 3538944 | tf_op jit(solution)/shard_map/all_gather | solution.py:186
  11.2 351.4 %all-gather.21.cloned.1.call-start = ((), (), s32[]{:S(2)}) async-start(), calls=%async_computation.14 | async-start | bytes 3538944 | tf_op jit(solution)/shard_map/all_gather | solution.py:202
  11.9 637.3 %reduce-scatter.8.cloned.1.call-start = ((), (), s32[]{:S(2)}) async-start(), calls=%async_computation.15 | async-start | bytes 1327104 | tf_op jit(solution)/shard_map/reduce_scatter | solution.py:326
  163.7 12.2 %copy-start.8 = (bf16[512,768]{0,1:T(8,128)(2,1)}, bf16[512,768]{0,1:T(8,128)(2,1)S(1)}, u32[]{:S(2)}) copy-start(bf16[512,768]{0,1:T(8,128)(2,1)S(1)} %copy.48) | copy-start | bytes 2359300
  185.3 116.4 %copy-start.17 = (bf16[512,768]{1,0:T(8,128)(2,1)}, bf16[512,768]{1,0:T(8,128)(2,1)S(1)}, u32[]{:S(2)}) copy-start(bf16[512,768]{1,0:T(8,128)(2,1)S(1)} %multiply_convert_fusion.5) | copy-start | bytes 2359300
  246.6 116.0 %copy-start.19 = (bf16[512,768]{1,0:T(8,128)(2,1)S(1)}, bf16[512,768]{1,0:T(8,128)(2,1)}, u32[]{:S(2)}) copy-start(bf16[512,768]{1,0:T(8,128)(2,1)} %param.27) | copy-start | bytes 2359300
  381.6 11.6 %slice-start.1 = ((s8[12582912]{0:T(1024)(128)(4,1)}), s8[4194304]{0:T(1024)(128)(4,1)S(1)}, s32[]{:S(2)}) async-start(s8[12582912]{0:T(1024)(128)(4,1)} %bitcast.75), calls=%async_computation.24 | async-start | bytes 8388608
  381.6 12.8 %slice-start.2 = ((s8[12582912]{0:T(1024)(128)(4,1)}), s8[4194304]{0:T(1024)(128)(4,1)S(1)}, s32[]{:S(2)}) async-start(s8[12582912]{0:T(1024)(128)(4,1)} %bitcast.75), calls=%async_computation.25 | async-start | bytes 8388608
  407.0 242.2 %reduce-scatter.10.cloned.1.call-start = ((), (), s32[]{:S(2)}) async-start(), calls=%async_computation.16 | async-start | bytes 1327104 | tf_op jit(solution)/shard_map/reduce_scatter | solution.py:329
  415.1 234.1 %reduce-scatter.12.cloned.1.call-start = ((), (), s32[]{:S(2)}) async-start(), calls=%async_computation.17 | async-start | bytes 1327104 | tf_op jit(solution)/shard_map/reduce_scatter | solution.py:332
  424.7 277.5 %reduce-scatter.14.cloned.1.call-start = ((), (), s32[]{:S(2)}) async-start(), calls=%async_computation.18 | async-start | bytes 1327104 | tf_op jit(solution)/shard_map/reduce_scatter | solution.py:335
  426.6 352.4 %reduce-scatter.16.cloned.1.call-start = ((), (), s32[]{:S(2)}) async-start(), calls=%async_computation.19 | async-start | bytes 3538944 | tf_op jit(solution)/shard_map/reduce_scatter | solution.py:338
  432.0 423.8 %reduce-scatter.18.cloned.1.call-start = ((), (), s32[]{:S(2)}) async-start(), calls=%async_computation.20 | async-start | bytes 3538944 | tf_op jit(solution)/shard_map/reduce_scatter | solution.py:341
  438.3 494.6 %reduce-scatter.20.cloned.1.call-start = ((), (), s32[]{:S(2)}) async-start(), calls=%async_computation.21 | async-start | bytes 3538944 | tf_op jit(solution)/shard_map/reduce_scatter | solution.py:344
  447.3 488.3 %all-to-all-start = ((bf16[8,256,768]{2,1,0:T(8,128)(2,1)}), bf16[8,256,768]{2,1,0:T(8,128)(2,1)}, u32[]{:S(2)}, u32[]{:S(2)}) async-start(bf16[8,256,768]{2,1,0:T(8,128)(2,1)} %stack.2), calls=%async_computation | async-start | bytes 6291456 | tf_op jit(solution)/shard_map/all_to_all | solution.py:177
  451.8 529.1 %all-reduce.14.cloned.1.call-start = ((), (), s32[]{:S(2)}) async-start(), calls=%async_computation.22 | async-start | bytes 3538944 | tf_op jit(solution)/shard_map/psum | solution.py:358
  (30 other events, 115.4 us)
Sparse Core Ops, SparseCore 0:
  10.2 43.9 all-gather.8
  56.4 39.8 all-gather.10
  98.5 39.7 all-gather.12
  140.3 39.7 all-gather.14
  182.2 58.7 all-gather.16
  243.0 58.6 all-gather.18
  303.9 58.6 all-gather.20
  407.1 69.6 reduce-scatter.7
  480.2 87.6 reduce-scatter.9
  571.1 63.9 reduce-scatter.11
  638.5 63.6 reduce-scatter.13
  705.6 73.3 reduce-scatter.15
  782.6 73.2 reduce-scatter.17
  859.3 73.5 reduce-scatter.19
  935.6 45.3 all-reduce.13
